TPU v7x, 32 devices: a whole 2x2x4 slice. The times are simulated.
32 devices in a mesh: cuts: 2 (over x), rows: 16 (over z, y, core).
Axes of the slice: x: 2, y: 2, z: 4, core: 2. Of those that a mesh axis runs over, the one named last changes fastest.
Arguments:
- start_modes: float32 [2, 64, 512, 128], P('cuts', 'rows'), may hold values from -6 to 6
- contrast: float32 [2, 64, 512], P('cuts', 'rows'), may hold values from 0 to 1
- rotations: float32 [2, 2, 128, 128], P('cuts'), may hold values from -0.2 to 1.2, as said below
- ordering: int32 [2, 2, 128], P('cuts'), may hold values from 0 to 127, each once within a row
Outputs:
- modes: float32 [2, 64, 512, 128], P('cuts', 'rows')
- coupling: float32 [2, 128, 128], P('cuts', 'rows')
- rayleigh: float32 [2, 128, 128], P('cuts', 'rows')
Inputs may be any that keep to these rules, and one draw needn't show every extreme that they name: `rotations`: each matrix is invertible.
All inputs are finite; a program needn't handle non-finite values.
Results may differ from a plain program's by a relative error of at most 0.00026.
Values sent between devices are 32-bit elements; how exact they have to be, the bound alone decides.
No kernel may reach another device: no remote copies, remote signals or barrier semaphores. Data moves between devices by JAX's collectives and lax.ppermute only.
A program may use at most 64 MiB of HBM per device.

v0:
```python
import jax
import jax.numpy as jnp
from jax import lax
from jax.sharding import PartitionSpec as P

DEGREE = 4
ITERS = 2


def padded_2(block, sides, width):
    for axis, dim in sides:
        count = lax.axis_size(axis)
        forward = [(i, i + 1) for i in range(count - 1)]
        backward = [(target, source) for source, target in forward]
        low = lax.ppermute(
            lax.slice_in_dim(block, block.shape[dim] - width, None, axis=dim), axis, forward
        )
        high = lax.ppermute(lax.slice_in_dim(block, 0, width, axis=dim), axis, backward)
        block = jnp.concatenate([low, block, high], axis=dim)
    return block


def from_behind(value, axis, by):
    peers = lax.axis_size(axis)
    pairs = [(i, i + by) for i in range(peers) if 0 <= i + by < peers]
    return lax.ppermute(value, axis, pairs)


def neighbour_sum(center, rows_source):
    columns = jnp.pad(center, ((0, 0), (1, 1), (0, 0)))
    return rows_source[2:] + rows_source[:-2] + columns[:, 2:] + columns[:, :-2]


def operator_core(center, rows_source, section):
    return (
        0.8 * (section[:, :, None] * center + 0.25 * neighbour_sum(center, rows_source))
        - 0.2 * center
    )


def inner_modes(left, right):
    return jnp.einsum("rcm,rcn->mn", left, right, precision=lax.Precision.HIGHEST)


def apply_edge(vectors, section):
    padded = padded_2(vectors, (("rows", 0),), 1)
    return operator_core(vectors, padded, section)


def body(start_modes, contrast, rotations, ordering):
    subspace = start_modes[0]
    section = contrast[0]
    turnings = rotations[0]
    sequence = ordering[0]
    rows_here = subspace.shape[0]
    columns = subspace.shape[1]
    nmodes = subspace.shape[2]
    tiles = lax.axis_size("rows")
    pixels = rows_here * tiles * columns
    wide_section = padded_2(section, (("rows", 0),), DEGREE)
    global_row = (
        lax.axis_index("rows") * rows_here
        + jnp.arange(rows_here + 2 * DEGREE, dtype=jnp.int32)
        - DEGREE
    )
    inside = ((global_row >= 0) & (global_row < rows_here * tiles)).astype(jnp.float32)[
        :, None, None
    ]
    for sweep in range(ITERS):

        def apply_local(vectors):
            return (
                operator_core(vectors, jnp.pad(vectors, ((1, 1), (0, 0), (0, 0))), wide_section)
                * inside
            )

        before = padded_2(subspace, (("rows", 0),), DEGREE)
        current = apply_local(before)
        for degree_step in range(2, DEGREE + 1):
            following = 2.0 * apply_local(current) - before
            before, current = (current, following)
        filtered = current[DEGREE : DEGREE + rows_here]
        gram_sum = lax.psum(inner_modes(filtered, filtered), "rows") / pixels
        factor_low = jnp.linalg.cholesky(gram_sum)
        mixing = lax.linalg.triangular_solve(
            factor_low, turnings[sweep], left_side=True, lower=True, transpose_a=True
        )
        picker = (sequence[sweep][None, :] == jnp.arange(nmodes, dtype=jnp.int32)[:, None]).astype(
            jnp.float32
        )
        mixing = jnp.dot(mixing, picker, precision=lax.Precision.HIGHEST)
        subspace = jnp.einsum("rcm,mn->rcn", filtered, mixing, precision=lax.Precision.HIGHEST)
    earlier = from_behind(subspace, "cuts", 1)
    earlier = jnp.where(lax.axis_index("cuts") == 0, start_modes[0], earlier)
    applied = apply_edge(subspace, section)
    coupling_term = inner_modes(earlier, subspace)
    rayleigh_term = inner_modes(subspace, applied)
    share_rows = nmodes // tiles
    coupling_sum, rayleigh_sum = lax.psum((coupling_term, rayleigh_term), "rows")
    coupling_part = lax.dynamic_slice_in_dim(
        coupling_sum, lax.axis_index("rows") * share_rows, share_rows, 0
    )
    rayleigh_part = lax.dynamic_slice_in_dim(
        rayleigh_sum, lax.axis_index("rows") * share_rows, share_rows, 0
    )
    return (subspace[None], (coupling_part / pixels)[None], (rayleigh_part / pixels)[None])


def solution(mesh):
    placed = (
        P("cuts", "rows", None, None),
        P("cuts", "rows", None),
        P("cuts", None, None, None),
        P("cuts", None, None),
    )
    return jax.shard_map(
        body,
        mesh=mesh,
        in_specs=placed,
        out_specs=(P("cuts", "rows", None, None), P("cuts", "rows", None), P("cuts", "rows", None)),
        check_vma=False,
    )
```

profile of v0, /device:TPU:8, one launch (start us, length us, event | category | flops | bytes accessed | tf_op | source)
XLA Modules:
  0.0 448.9 jit_solution(6304230805131383144)
XLA Ops:
  7.2 2.8 collective-permute-start.3
  11.9 4.5 %collective-permute-start.1 = (f32[4,512]{1,0:T(4,128)}, f32[4,512]{1,0:T(4,128)S(1)}, u32[]{:S(2)}, u32[]{:S(2)}) collective-permute-start(f32[4,512]{1,0:T(4,128)} %bitcast.65), channel_id=1, source_target_pairs={{1,0},{2,1},{3,2},{4,3},{5,4},{6,5},{7,6},{8,7},{9,8},{10,9},{11,1... | collective-permute-start | bytes 24584 | tf_op jit(solution)/shard_map/ppermute | solution.py:18
  18.4 4.2 collective-permute-done.1
  22.6 4.8 %collective-permute-done = f32[4,512]{1,0:T(4,128)S(1)} collective-permute-done((f32[4,512]{1,0:T(4,128)}, f32[4,512]{1,0:T(4,128)S(1)}, u32[]{:S(2)}, u32[]{:S(2)}) %collective-permute-start) | collective-permute-done | bytes 8224 | tf_op jit(solution)/shard_map/ppermute | solution.py:15
  31.5 2.7 fusion.17
  34.2 4.0 fusion.27
  43.1 97.2 %all-reduce.22.cloned.1.call-done = f32[128,128]{0,1:T(8,128)} async-done(((f32[128,128]{0,1:T(8,128)}), f32[128,128]{0,1:T(8,128)}) %all-reduce.22.cloned.1.call-update) | async-done | bytes 65552 | tf_op jit(solution)/shard_map/psum | solution.py:83
  142.1 11.7 %cholesky.44 = f32[128,128]{1,0:T(8,128)S(1)} custom-call(f32[128,128]{1,0:T(8,128)S(1)} %fusion.108), custom_call_target="Cholesky" | custom-call | tf_op jit(solution)/shard_map/jit(cholesky)/cholesky | solution.py:84
  155.1 9.8 %custom-call.6 = f32[1,128,128]{1,2,0:T(8,128)S(1)} custom-call(f32[1,128,128]{2,1,0:T(8,128)S(1)} %fusion.99), custom_call_target="InvertDiagBlocksLowerTriangular" | custom-call | tf_op jit(solution)/shard_map/triangular_solve/custom-call.0 | solution.py:85
  168.2 2.6 collective-permute-start.4
  170.9 9.7 %collective-permute-done.5 = f32[4,512,128]{2,1,0:T(8,128)S(1)} collective-permute-done((f32[4,512,128]{2,1,0:T(8,128)S(1)}, f32[4,512,128]{2,1,0:T(8,128)S(1)}, u32[]{:S(2)}, u32[]{:S(2)}) %collective-permute-start.5) | collective-permute-done | bytes 1048608 | tf_op jit(solution)/shard_map/ppermute | solution.py:18
  180.6 4.8 %collective-permute-done.4 = f32[4,512,128]{2,1,0:T(8,128)S(1)} collective-permute-done((f32[4,512,128]{2,1,0:T(8,128)S(1)}, f32[4,512,128]{2,1,0:T(8,128)S(1)}, u32[]{:S(2)}, u32[]{:S(2)}) %collective-permute-start.4) | collective-permute-done | bytes 1048608 | tf_op jit(solution)/shard_map/ppermute | solution.py:15
  187.6 2.7 fusion.55
  190.2 4.0 fusion.65
  196.4 2.4 convolution_bitcast_fusion
  198.9 96.1 %all-reduce.24.cloned.1.call-done = f32[128,128]{0,1:T(8,128)} async-done(((f32[128,128]{0,1:T(8,128)}), f32[128,128]{0,1:T(8,128)}) %all-reduce.24.cloned.1.call-update) | async-done | bytes 65552 | tf_op jit(solution)/shard_map/psum | solution.py:83
  296.9 11.7 %cholesky.55 = f32[128,128]{1,0:T(8,128)S(1)} custom-call(f32[128,128]{1,0:T(8,128)S(1)} %fusion.104), custom_call_target="Cholesky" | custom-call | tf_op jit(solution)/shard_map/jit(cholesky)/cholesky | solution.py:84
  309.9 9.8 %custom-call.7 = f32[1,128,128]{1,2,0:T(8,128)S(1)} custom-call(f32[1,128,128]{2,1,0:T(8,128)S(1)} %fusion.100), custom_call_target="InvertDiagBlocksLowerTriangular" | custom-call | tf_op jit(solution)/shard_map/triangular_solve/custom-call.0 | solution.py:85
  322.1 3.6 collective-permute-start.6
  328.6 2.7 collective-permute-start.8
  332.6 4.7 %collective-permute-done.8 = f32[1,512,128]{2,1,0:T(8,128)S(1)} collective-permute-done((f32[1,512,128]{2,1,0:T(8,128)S(1)}, f32[1,512,128]{2,1,0:T(8,128)S(1)}, u32[]{:S(2)}, u32[]{:S(2)}) %collective-permute-start.8) | collective-permute-done | bytes 262176 | tf_op jit(solution)/shard_map/ppermute | solution.py:15
  337.2 6.2 %convolution_bitcast_fusion.2 = f32[128,128]{1,0:T(8,128)} fusion(f32[4,512,128]{2,1,0:T(8,128)} %fusion.121, f32[1,512,128]{2,1,0:T(8,128)S(1)} %collective-permute-done.8, f32[1,512,128]{2,1,0:T(8,128)S(1)} %collective-permute-done.7, f32[4,512]{1,0:T(4,128)S(1)} %bitcast.68), kind=kOutput, calls=%fused_computation.96 | convolution fusion | flops 405536768 | bytes 2695168 | tf_op jit(solution)/shard_map/rcm,rcn->mn/dot_general | solution.py:42
  345.1 3.7 convolution_bitcast_fusion.3
  348.8 92.3 %all-reduce.26.cloned.1.call-done = (f32[128,128]{1,0:T(8,128)}, f32[128,128]{1,0:T(8,128)}) async-done(((f32[128,128]{1,0:T(8,128)}, f32[128,128]{1,0:T(8,128)}), (f32[128,128]{1,0:T(8,128)}, f32[128,128]{1,0:T(8,128)})) %all-reduce.26.cloned.1.call-update) | async-done | bytes 131088 | tf_op jit(solution)/shard_map/psum | solution.py:99
  (54 shorter events, 36.2 us)
Async XLA Ops:
  7.2 133.1 %all-reduce.22.cloned.1.call-start = ((), (), s32[]{:S(2)}) async-start(), calls=%async_computation | async-start | bytes 131072 | tf_op jit(solution)/shard_map/psum | solution.py:83
  7.2 20.9 %collective-permute-start.3 = (f32[4,512,128]{2,1,0:T(8,128)}, f32[4,512,128]{2,1,0:T(8,128)S(1)}, u32[]{:S(2)}, u32[]{:S(2)}) collective-permute-start(f32[4,512,128]{2,1,0:T(8,128)} %bitcast.61), channel_id=1, source_target_pairs={{1,0},{2,1},{3,2},{4,3},{5,4},{6,5},{7,6},{8,7},{9,8},{10,9},{11,1... | collective-permute-start | bytes 3145736 | tf_op jit(solution)/shard_map/ppermute | solution.py:18
  10.0 18.1 %collective-permute-start.2 = (f32[4,512,128]{2,1,0:T(8,128)}, f32[4,512,128]{2,1,0:T(8,128)S(1)}, u32[]{:S(2)}, u32[]{:S(2)}) collective-permute-start(f32[4,512,128]{2,1,0:T(8,128)} %bitcast.62), channel_id=1, source_target_pairs={{0,1},{1,2},{2,3},{3,4},{4,5},{5,6},{6,7},{7,8},{8,9},{9,10},{10,1... | collective-permute-start | bytes 3145736 | tf_op jit(solution)/shard_map/ppermute | solution.py:15
  11.9 10.7 %collective-permute-start.1 = (f32[4,512]{1,0:T(4,128)}, f32[4,512]{1,0:T(4,128)S(1)}, u32[]{:S(2)}, u32[]{:S(2)}) collective-permute-start(f32[4,512]{1,0:T(4,128)} %bitcast.65), channel_id=1, source_target_pairs={{1,0},{2,1},{3,2},{4,3},{5,4},{6,5},{7,6},{8,7},{9,8},{10,9},{11,1... | collective-permute-start | bytes 24584 | tf_op jit(solution)/shard_map/ppermute | solution.py:18
  16.5 10.9 %collective-permute-start = (f32[4,512]{1,0:T(4,128)}, f32[4,512]{1,0:T(4,128)S(1)}, u32[]{:S(2)}, u32[]{:S(2)}) collective-permute-start(f32[4,512]{1,0:T(4,128)} %bitcast.66), channel_id=1, source_target_pairs={{0,1},{1,2},{2,3},{3,4},{4,5},{5,6},{6,7},{7,8},{8,9},{9,10},{10,1... | collective-permute-start | bytes 24584 | tf_op jit(solution)/shard_map/ppermute | solution.py:15
  29.6 2.0 copy-start
  40.3 2.7 copy-start.4
  40.3 124.6 %copy-start.2 = (f32[1,2,128,128]{3,2,1,0:T(8,128)S(1)}, f32[1,2,128,128]{3,2,1,0:T(8,128)}, u32[]{:S(2)}) copy-start(f32[1,2,128,128]{3,2,1,0:T(8,128)} %param.9) | copy-start | bytes 393220
  42.8 252.3 %all-reduce.24.cloned.1.call-start = ((), (), s32[]{:S(2)}) async-start(), calls=%async_computation.1 | async-start | bytes 131072 | tf_op jit(solution)/shard_map/psum | solution.py:83
  166.3 14.3 %collective-permute-start.5 = (f32[4,512,128]{2,1,0:T(8,128)S(1)}, f32[4,512,128]{2,1,0:T(8,128)S(1)}, u32[]{:S(2)}, u32[]{:S(2)}) collective-permute-start(f32[4,512,128]{2,1,0:T(8,128)S(1)} %fusion.120), channel_id=1, source_target_pairs={{1,0},{2,1},{3,2},{4,3},{5,4},{6,5},{7,6},{8,7},{9,8},{10,9},{11,1... | collective-permute-start | bytes 3145736 | tf_op jit(solution)/shard_map/ppermute | solution.py:18
  168.2 17.1 %collective-permute-start.4 = (f32[4,512,128]{2,1,0:T(8,128)S(1)}, f32[4,512,128]{2,1,0:T(8,128)S(1)}, u32[]{:S(2)}, u32[]{:S(2)}) collective-permute-start(f32[4,512,128]{2,1,0:T(8,128)S(1)} %fusion.120), channel_id=1, source_target_pairs={{0,1},{1,2},{2,3},{3,4},{4,5},{5,6},{6,7},{7,8},{8,9},{9,10},{10,1... | collective-permute-start | bytes 3145736 | tf_op jit(solution)/shard_map/ppermute | solution.py:15
  196.4 140.8 %copy-start.3 = (f32[1,4,512]{2,1,0:T(4,128)S(1)}, f32[1,4,512]{2,1,0:T(4,128)}, u32[]{:S(2)}) copy-start(f32[1,4,512]{2,1,0:T(4,128)} %param.8) | copy-start | bytes 24580
  198.9 242.2 %all-reduce.26.cloned.1.call-start = ((), (), s32[]{:S(2)}) async-start(), calls=%async_computation.2 | async-start | bytes 262144 | tf_op jit(solution)/shard_map/psum | solution.py:99
  322.1 23.0 %copy-start.1 = (f32[1,4,512,128]{3,2,1,0:T(8,128)S(1)}, f32[1,4,512,128]{3,2,1,0:T(8,128)}, u32[]{:S(2)}) copy-start(f32[1,4,512,128]{3,2,1,0:T(8,128)} %param.7) | copy-start | bytes 3145732
  322.1 23.0 %collective-permute-start.6 = (f32[4,512,128]{2,1,0:T(8,128)}, f32[4,512,128]{2,1,0:T(8,128)S(1)}, u32[]{:S(2)}, u32[]{:S(2)}) collective-permute-start(f32[4,512,128]{2,1,0:T(8,128)} %fusion.121), channel_id=1, source_target_pairs={{0,16},{1,17},{2,18},{3,19},{4,20},{5,21},{6,22},{7,23},{8,24},{9,... | collective-permute-start | bytes 3145736 | tf_op jit(solution)/shard_map/ppermute | solution.py:26
  326.7 5.8 %collective-permute-start.7 = (f32[1,512,128]{2,1,0:T(8,128)S(1)}, f32[1,512,128]{2,1,0:T(8,128)S(1)}, u32[]{:S(2)}, u32[]{:S(2)}) collective-permute-start(f32[1,512,128]{2,1,0:T(8,128)S(1)} %get-tuple-element.7), channel_id=1, source_target_pairs={{1,0},{2,1},{3,2},{4,3},{5,4},{6,5},{7,6},{8,7},{9,8},{10,9},{11,1... | collective-permute-start | bytes 786440 | tf_op jit(solution)/shard_map/ppermute | solution.py:18
  328.6 8.6 %collective-permute-start.8 = (f32[1,512,128]{2,1,0:T(8,128)S(1)}, f32[1,512,128]{2,1,0:T(8,128)S(1)}, u32[]{:S(2)}, u32[]{:S(2)}) collective-permute-start(f32[1,512,128]{2,1,0:T(8,128)S(1)} %get-tuple-element.8), channel_id=1, source_target_pairs={{0,1},{1,2},{2,3},{3,4},{4,5},{5,6},{6,7},{7,8},{8,9},{9,10},{10,1... | collective-permute-start | bytes 786440 | tf_op jit(solution)/shard_map/ppermute | solution.py:15
Sparse Core Ops, SparseCore 0:
  42.9 97.2 all-reduce.21
  199.0 96.0 all-reduce.23
  348.9 92.1 all-reduce.25
where the time goes:
time: 450 us; the launch traced here: 449 us
  waiting for transfers between devices  317 us (70%)
  other arithmetic  74.2 us (16%)
  starting transfers between devices  24.1 us (5%)
  matrix products  18.5 us (4%)
  between operations  14.1 us (3%)
    psum x2, waiting for transfers between devices, body(): gram_sum = lax.psum(inner_modes(filtered, filtered), 'rows') / pixels  193 us
    psum x1, waiting for transfers between devices, body(): lax.psum((coupling_term, rayleigh_term), 'rows')  92.3 us
    another operation x6, other arithmetic, body(): factor_low = jnp.linalg.cholesky(gram_sum)  24.8 us
    another operation x4, other arithmetic, body(): lax.linalg.triangular_solve(factor_low, turnings[sweep], left_side=True,...  20.9 us
    sub x6, other arithmetic, body(): following = 2.0 * apply_local(current) - before  17.6 us
    ppermute x4, waiting for transfers between devices, padded_2(): lax.ppermute(lax.slice_in_dim(block, 0, width, axis=dim), axis, backward)  15.2 us
    dot_general x4, matrix products, inner_modes(): jnp.einsum('rcm,rcn->mn', left, right, precision=lax.Precision.HIGHEST)  14.8 us
    ppermute x4, waiting for transfers between devices, padded_2(): lax.ppermute(lax.slice_in_dim(block, block.shape[dim] - width, None, axis...  14.2 us
  transfers between devices with their start and end apart: 12, of which 10 were waited for; matrix products, arithmetic and copies ran while one was open for 2% of the time, Pallas kernels for 0%

commit v1 on v0

--- a/solution.py
+++ b/solution.py
@@ -80,7 +80,7 @@
             following = 2.0 * apply_local(current) - before
             before, current = (current, following)
         filtered = current[DEGREE : DEGREE + rows_here]
-        gram_sum = lax.psum(inner_modes(filtered, filtered), "rows") / pixels
+        gram_sum = jnp.sum(lax.all_gather(inner_modes(filtered, filtered), "rows"), axis=0) / pixels
         factor_low = jnp.linalg.cholesky(gram_sum)
         mixing = lax.linalg.triangular_solve(
             factor_low, turnings[sweep], left_side=True, lower=True, transpose_a=True

time: 450 us -> 350 us (0.78)
  waiting for transfers between devices: 317 us -> 217 us
    psum x2 -> x0, waiting for transfers between devices: 193 us -> none  [body(): gram_sum = lax.psum(inner_modes(filtered, filtered), 'rows') / pixels]
    all_gather x0 -> x2, waiting for transfers between devices: none -> 89.7 us  [body(): lax.all_gather(inner_modes(filtered, filtered), 'rows')]
where the time goes in v1:
time: 350 us; the launch traced here: 349 us
  waiting for transfers between devices  217 us (62%)
  other arithmetic  73.4 us (21%)
  starting transfers between devices  25.1 us (7%)
  matrix products  18.4 us (5%)
  between operations  14.1 us (4%)
    psum x1, waiting for transfers between devices, body(): lax.psum((coupling_term, rayleigh_term), 'rows')  92 us
    all_gather x2, waiting for transfers between devices, body(): lax.all_gather(inner_modes(filtered, filtered), 'rows')  89.7 us
    another operation x6, other arithmetic, body(): factor_low = jnp.linalg.cholesky(gram_sum)  24.8 us
    another operation x4, other arithmetic, body(): lax.linalg.triangular_solve(factor_low, turnings[sweep], left_side=True,...  20.9 us
    sub x6, other arithmetic, body(): following = 2.0 * apply_local(current) - before  17.6 us
    ppermute x4, waiting for transfers between devices, padded_2(): lax.ppermute(lax.slice_in_dim(block, 0, width, axis=dim), axis, backward)  16.3 us
    dot_general x4, matrix products, inner_modes(): jnp.einsum('rcm,rcn->mn', left, right, precision=lax.Precision.HIGHEST)  14.7 us
    ppermute x4, waiting for transfers between devices, padded_2(): lax.ppermute(lax.slice_in_dim(block, block.shape[dim] - width, None, axis...  14.3 us
  transfers between devices with their start and end apart: 12, of which 10 were waited for; matrix products, arithmetic and copies ran while one was open for 2% of the time, Pallas kernels for 0%

profile of v1, /device:TPU:8, one launch (start us, length us, event | category | flops | bytes accessed | tf_op | source)
XLA Modules:
  0.0 349.3 jit_solution(14084883820328481354)
XLA Ops:
  7.2 2.8 collective-permute-start.3
  11.9 4.5 %collective-permute-start.1 = (f32[4,512]{1,0:T(4,128)}, f32[4,512]{1,0:T(4,128)S(1)}, u32[]{:S(2)}, u32[]{:S(2)}) collective-permute-start(f32[4,512]{1,0:T(4,128)} %bitcast.69), channel_id=1, source_target_pairs={{1,0},{2,1},{3,2},{4,3},{5,4},{6,5},{7,6},{8,7},{9,8},{10,9},{11,1... | collective-permute-start | bytes 24584 | tf_op jit(solution)/shard_map/ppermute | solution.py:18
  18.4 4.2 %collective-permute-done.1 = f32[4,512]{1,0:T(4,128)S(1)} collective-permute-done((f32[4,512]{1,0:T(4,128)}, f32[4,512]{1,0:T(4,128)S(1)}, u32[]{:S(2)}, u32[]{:S(2)}) %collective-permute-start.1) | collective-permute-done | bytes 8224 | tf_op jit(solution)/shard_map/ppermute | solution.py:18
  22.6 4.8 %collective-permute-done = f32[4,512]{1,0:T(4,128)S(1)} collective-permute-done((f32[4,512]{1,0:T(4,128)}, f32[4,512]{1,0:T(4,128)S(1)}, u32[]{:S(2)}, u32[]{:S(2)}) %collective-permute-start) | collective-permute-done | bytes 8224 | tf_op jit(solution)/shard_map/ppermute | solution.py:15
  31.5 2.7 fusion.17
  34.2 4.0 %fusion.27 = f32[12,512,128]{2,1,0:T(8,128)S(1)} fusion(f32[12,512,128]{2,1,0:T(8,128)S(1)} %fusion.17, f32[12]{0:T(128)S(1)} %and_convert_fusion, f32[12,512]{1,0:T(8,128)S(1)} %pad_maximum_fusion.5, f32[12,512,128]{2,1,0:T(8,128)S(1)} %pad_maximum_fusion), kind=kLoop, calls=%fused_computation.43 | loop fusion | flops 17301504 | bytes 9461808 | tf_op jit(solution)/shard_map/sub | solution.py:80
  43.1 45.4 %all-gather.5.cloned.1.call-done = f32[2048,128]{1,0:T(8,128)} async-done(((f32[128,128]{1,0:T(8,128)}), f32[2048,128]{1,0:T(8,128)}) %all-gather.5.cloned.1.call-update) | async-done | bytes 1048592 | tf_op jit(solution)/shard_map/all_gather | solution.py:83
  90.0 11.7 %cholesky.44 = f32[128,128]{1,0:T(8,128)S(1)} custom-call(f32[128,128]{1,0:T(8,128)S(1)} %fusion.108), custom_call_target="Cholesky" | custom-call | tf_op jit(solution)/shard_map/jit(cholesky)/cholesky | solution.py:84
  103.0 9.8 %custom-call.6 = f32[1,128,128]{1,2,0:T(8,128)S(1)} custom-call(f32[1,128,128]{2,1,0:T(8,128)S(1)} %fusion.99), custom_call_target="InvertDiagBlocksLowerTriangular" | custom-call | tf_op jit(solution)/shard_map/triangular_solve/custom-call.0 | solution.py:85
  114.2 3.2 collective-permute-start.5
  119.6 10.2 %collective-permute-done.5 = f32[4,512,128]{2,1,0:T(8,128)S(1)} collective-permute-done((f32[4,512,128]{2,1,0:T(8,128)S(1)}, f32[4,512,128]{2,1,0:T(8,128)S(1)}, u32[]{:S(2)}, u32[]{:S(2)}) %collective-permute-start.5) | collective-permute-done | bytes 1048608 | tf_op jit(solution)/shard_map/ppermute | solution.py:18
  129.8 4.8 %collective-permute-done.4 = f32[4,512,128]{2,1,0:T(8,128)S(1)} collective-permute-done((f32[4,512,128]{2,1,0:T(8,128)S(1)}, f32[4,512,128]{2,1,0:T(8,128)S(1)}, u32[]{:S(2)}, u32[]{:S(2)}) %collective-permute-start.4) | collective-permute-done | bytes 1048608 | tf_op jit(solution)/shard_map/ppermute | solution.py:15
  136.7 2.7 fusion.55
  139.4 4.0 %fusion.65 = f32[12,512,128]{2,1,0:T(8,128)S(1)} fusion(f32[12,512,128]{2,1,0:T(8,128)S(1)} %fusion.55, f32[12]{0:T(128)S(1)} %and_convert_fusion, f32[12,512]{1,0:T(8,128)S(1)} %pad_maximum_fusion.5, f32[12,512,128]{2,1,0:T(8,128)S(1)} %pad_maximum_fusion.1), kind=kLoop, calls=%fused_computation.81 | loop fusion | flops 17301504 | bytes 9461808 | tf_op jit(solution)/shard_map/sub | solution.py:80
  148.1 44.4 %all-gather.7.cloned.1.call-done = f32[2048,128]{1,0:T(8,128)} async-done(((f32[128,128]{1,0:T(8,128)}), f32[2048,128]{1,0:T(8,128)}) %all-gather.7.cloned.1.call-update) | async-done | bytes 1048592 | tf_op jit(solution)/shard_map/all_gather | solution.py:83
  194.0 11.7 %cholesky.55 = f32[128,128]{1,0:T(8,128)S(1)} custom-call(f32[128,128]{1,0:T(8,128)S(1)} %fusion.104), custom_call_target="Cholesky" | custom-call | tf_op jit(solution)/shard_map/jit(cholesky)/cholesky | solution.py:84
  207.0 9.8 %custom-call.7 = f32[1,128,128]{1,2,0:T(8,128)S(1)} custom-call(f32[1,128,128]{2,1,0:T(8,128)S(1)} %fusion.100), custom_call_target="InvertDiagBlocksLowerTriangular" | custom-call | tf_op jit(solution)/shard_map/triangular_solve/custom-call.0 | solution.py:85
  219.2 3.6 %collective-permute-start.6 = (f32[4,512,128]{2,1,0:T(8,128)}, f32[4,512,128]{2,1,0:T(8,128)S(1)}, u32[]{:S(2)}, u32[]{:S(2)}) collective-permute-start(f32[4,512,128]{2,1,0:T(8,128)} %fusion.121), channel_id=1, source_target_pairs={{0,16},{1,17},{2,18},{3,19},{4,20},{5,21},{6,22},{7,23},{8,24},{9,... | collective-permute-start | bytes 3145736 | tf_op jit(solution)/shard_map/ppermute | solution.py:26
  223.8 2.9 collective-permute-start.7
  230.6 4.7 %collective-permute-done.8 = f32[1,512,128]{2,1,0:T(8,128)S(1)} collective-permute-done((f32[1,512,128]{2,1,0:T(8,128)S(1)}, f32[1,512,128]{2,1,0:T(8,128)S(1)}, u32[]{:S(2)}, u32[]{:S(2)}) %collective-permute-start.8) | collective-permute-done | bytes 262176 | tf_op jit(solution)/shard_map/ppermute | solution.py:15
  235.3 6.2 %convolution_bitcast_fusion.2 = f32[128,128]{1,0:T(8,128)} fusion(f32[4,512,128]{2,1,0:T(8,128)} %fusion.121, f32[1,512,128]{2,1,0:T(8,128)S(1)} %collective-permute-done.8, f32[1,512,128]{2,1,0:T(8,128)S(1)} %collective-permute-done.7, f32[4,512]{1,0:T(4,128)S(1)} %bitcast.72), kind=kOutput, calls=%fused_computation.96 | convolution fusion | flops 405536768 | bytes 2695168 | tf_op jit(solution)/shard_map/rcm,rcn->mn/dot_general | solution.py:42
  241.5 4.3 %collective-permute-done.6 = f32[4,512,128]{2,1,0:T(8,128)S(1)} collective-permute-done((f32[4,512,128]{2,1,0:T(8,128)}, f32[4,512,128]{2,1,0:T(8,128)S(1)}, u32[]{:S(2)}, u32[]{:S(2)}) %collective-permute-start.6) | collective-permute-done | bytes 1048608 | tf_op jit(solution)/shard_map/ppermute | solution.py:26
  245.8 3.7 %convolution_bitcast_fusion.3 = f32[128,128]{1,0:T(8,128)} fusion(f32[4,512,128]{2,1,0:T(8,128)} %fusion.121, f32[4,512,128]{2,1,0:T(8,128)S(1)} %collective-permute-done.6, pred[]{:T(512)S(6)} %eq.41, f32[1,4,512,128]{3,2,1,0:T(8,128)S(1)} %copy-done.1), kind=kOutput, calls=%fused_computation.97 | convolution fusion | flops 402915328 | bytes 3211265 | tf_op jit(solution)/shard_map/rcm,rcn->mn/dot_general | solution.py:42
  249.5 92.0 %all-reduce.20.cloned.1.call-done = (f32[128,128]{1,0:T(8,128)}, f32[128,128]{1,0:T(8,128)}) async-done(((f32[128,128]{1,0:T(8,128)}, f32[128,128]{1,0:T(8,128)}), (f32[128,128]{1,0:T(8,128)}, f32[128,128]{1,0:T(8,128)})) %all-reduce.20.cloned.1.call-update) | async-done | bytes 131088 | tf_op jit(solution)/shard_map/psum | solution.py:99
  (58 shorter events, 37.3 us)
Async XLA Ops:
  7.2 81.3 %all-gather.5.cloned.1.call-start = ((), (), s32[]{:S(2)}) async-start(), calls=%async_computation | async-start | bytes 1114112 | tf_op jit(solution)/shard_map/all_gather | solution.py:83
  7.2 20.9 %collective-permute-start.3 = (f32[4,512,128]{2,1,0:T(8,128)}, f32[4,512,128]{2,1,0:T(8,128)S(1)}, u32[]{:S(2)}, u32[]{:S(2)}) collective-permute-start(f32[4,512,128]{2,1,0:T(8,128)} %bitcast.63), channel_id=1, source_target_pairs={{1,0},{2,1},{3,2},{4,3},{5,4},{6,5},{7,6},{8,7},{9,8},{10,9},{11,1... | collective-permute-start | bytes 3145736 | tf_op jit(solution)/shard_map/ppermute | solution.py:18
  10.0 18.1 %collective-permute-start.2 = (f32[4,512,128]{2,1,0:T(8,128)}, f32[4,512,128]{2,1,0:T(8,128)S(1)}, u32[]{:S(2)}, u32[]{:S(2)}) collective-permute-start(f32[4,512,128]{2,1,0:T(8,128)} %bitcast.64), channel_id=1, source_target_pairs={{0,1},{1,2},{2,3},{3,4},{4,5},{5,6},{6,7},{7,8},{8,9},{9,10},{10,1... | collective-permute-start | bytes 3145736 | tf_op jit(solution)/shard_map/ppermute | solution.py:15
  11.9 10.7 %collective-permute-start.1 = (f32[4,512]{1,0:T(4,128)}, f32[4,512]{1,0:T(4,128)S(1)}, u32[]{:S(2)}, u32[]{:S(2)}) collective-permute-start(f32[4,512]{1,0:T(4,128)} %bitcast.69), channel_id=1, source_target_pairs={{1,0},{2,1},{3,2},{4,3},{5,4},{6,5},{7,6},{8,7},{9,8},{10,9},{11,1... | collective-permute-start | bytes 24584 | tf_op jit(solution)/shard_map/ppermute | solution.py:18
  16.5 10.9 %collective-permute-start = (f32[4,512]{1,0:T(4,128)}, f32[4,512]{1,0:T(4,128)S(1)}, u32[]{:S(2)}, u32[]{:S(2)}) collective-permute-start(f32[4,512]{1,0:T(4,128)} %bitcast.70), channel_id=1, source_target_pairs={{0,1},{1,2},{2,3},{3,4},{4,5},{5,6},{6,7},{7,8},{8,9},{9,10},{10,1... | collective-permute-start | bytes 24584 | tf_op jit(solution)/shard_map/ppermute | solution.py:15
  29.6 2.0 copy-start
  40.3 2.7 copy-start.4
  40.3 72.5 %copy-start.2 = (f32[1,2,128,128]{3,2,1,0:T(8,128)S(1)}, f32[1,2,128,128]{3,2,1,0:T(8,128)}, u32[]{:S(2)}) copy-start(f32[1,2,128,128]{3,2,1,0:T(8,128)} %param.9) | copy-start | bytes 393220
  42.8 149.6 %all-gather.7.cloned.1.call-start = ((), (), s32[]{:S(2)}) async-start(), calls=%async_computation.1 | async-start | bytes 1114112 | tf_op jit(solution)/shard_map/all_gather | solution.py:83
  114.2 15.5 %collective-permute-start.5 = (f32[4,512,128]{2,1,0:T(8,128)S(1)}, f32[4,512,128]{2,1,0:T(8,128)S(1)}, u32[]{:S(2)}, u32[]{:S(2)}) collective-permute-start(f32[4,512,128]{2,1,0:T(8,128)S(1)} %fusion.120), channel_id=1, source_target_pairs={{1,0},{2,1},{3,2},{4,3},{5,4},{6,5},{7,6},{8,7},{9,8},{10,9},{11,1... | collective-permute-start | bytes 3145736 | tf_op jit(solution)/shard_map/ppermute | solution.py:18
  117.4 17.1 %collective-permute-start.4 = (f32[4,512,128]{2,1,0:T(8,128)S(1)}, f32[4,512,128]{2,1,0:T(8,128)S(1)}, u32[]{:S(2)}, u32[]{:S(2)}) collective-permute-start(f32[4,512,128]{2,1,0:T(8,128)S(1)} %fusion.120), channel_id=1, source_target_pairs={{0,1},{1,2},{2,3},{3,4},{4,5},{5,6},{6,7},{7,8},{8,9},{9,10},{10,1... | collective-permute-start | bytes 3145736 | tf_op jit(solution)/shard_map/ppermute | solution.py:15
  148.0 87.3 %copy-start.3 = (f32[1,4,512]{2,1,0:T(4,128)S(1)}, f32[1,4,512]{2,1,0:T(4,128)}, u32[]{:S(2)}) copy-start(f32[1,4,512]{2,1,0:T(4,128)} %param.8) | copy-start | bytes 24580
  148.0 193.5 %all-reduce.20.cloned.1.call-start = ((), (), s32[]{:S(2)}) async-start(), calls=%async_computation.2 | async-start | bytes 262144 | tf_op jit(solution)/shard_map/psum | solution.py:99
  219.2 26.6 %copy-start.1 = (f32[1,4,512,128]{3,2,1,0:T(8,128)S(1)}, f32[1,4,512,128]{3,2,1,0:T(8,128)}, u32[]{:S(2)}) copy-start(f32[1,4,512,128]{3,2,1,0:T(8,128)} %param.7) | copy-start | bytes 3145732
  219.2 26.6 %collective-permute-start.6 = (f32[4,512,128]{2,1,0:T(8,128)}, f32[4,512,128]{2,1,0:T(8,128)S(1)}, u32[]{:S(2)}, u32[]{:S(2)}) collective-permute-start(f32[4,512,128]{2,1,0:T(8,128)} %fusion.121), channel_id=1, source_target_pairs={{0,16},{1,17},{2,18},{3,19},{4,20},{5,21},{6,22},{7,23},{8,24},{9,... | collective-permute-start | bytes 3145736 | tf_op jit(solution)/shard_map/ppermute | solution.py:26
  223.8 6.8 %collective-permute-start.7 = (f32[1,512,128]{2,1,0:T(8,128)S(1)}, f32[1,512,128]{2,1,0:T(8,128)S(1)}, u32[]{:S(2)}, u32[]{:S(2)}) collective-permute-start(f32[1,512,128]{2,1,0:T(8,128)S(1)} %get-tuple-element.7), channel_id=1, source_target_pairs={{1,0},{2,1},{3,2},{4,3},{5,4},{6,5},{7,6},{8,7},{9,8},{10,9},{11,1... | collective-permute-start | bytes 786440 | tf_op jit(solution)/shard_map/ppermute | solution.py:18
  226.7 8.6 %collective-permute-start.8 = (f32[1,512,128]{2,1,0:T(8,128)S(1)}, f32[1,512,128]{2,1,0:T(8,128)S(1)}, u32[]{:S(2)}, u32[]{:S(2)}) collective-permute-start(f32[1,512,128]{2,1,0:T(8,128)S(1)} %get-tuple-element.8), channel_id=1, source_target_pairs={{0,1},{1,2},{2,3},{3,4},{4,5},{5,6},{6,7},{7,8},{8,9},{9,10},{10,1... | collective-permute-start | bytes 786440 | tf_op jit(solution)/shard_map/ppermute | solution.py:15
Sparse Core Ops, SparseCore 0:
  42.9 45.4 all-gather.4
  148.2 44.2 all-gather.6
  249.6 91.8 all-reduce.19
